TPU v7x, 256 devices: a whole 4x4x8 slice. The times are simulated.
256 devices in a mesh: az: 32 (over x, z_hi, core), rad: 8 (over z_lo, y).
Axes of the slice: x: 4, y: 4, z: 8 (z_hi: 4, z_lo: 2; z = z_hi * 2 + z_lo), core: 2. Of those that a mesh axis runs over, the one named last changes fastest.
Arguments:
- fields: float32 [5, 8, 512, 4096], P(None, None, 'rad', 'az'), may hold values from -6 to 6
- velocity: float32 [8, 512, 4096], P(None, 'rad', 'az'), may hold values from -0.5 to 0.5
- shifts: int32 [512], P('rad'), may hold values from 0 to 4095, as said below
- block_inverse: float32 [8, 512, 64], P(None, 'rad'), may hold values from -1 to 1, as said below
- coupling: float32 [8, 8], P(None, 'rad'), may hold values from 0.2 to 0.5
Outputs:
- updated: float32 [5, 8, 512, 4096], P(None, None, 'rad', 'az')
Inputs may be any that keep to these rules, and one draw needn't show every extreme that they name: `shifts`: each radius's shift; the values 0 and 4095 both occur in every draw. `block_inverse`: entries of the given block inverses.
All inputs are finite; a program needn't handle non-finite values.
Results may differ from a plain program's by a relative error of at most 0.000075.
Values sent between devices are 32-bit elements; how exact they have to be, the bound alone decides.
A program may use at most 256 MiB of HBM per device.

v0:
```python
import jax
import jax.numpy as jnp
from jax import lax
from jax.sharding import PartitionSpec as P


def shifted(block, axis, distance):
    devices = range(lax.axis_size(axis))
    route = [((i - distance) % len(devices), i) for i in devices]
    return lax.ppermute(block, axis, route)


def extended(shard, sides, width):
    for axis, dim in sides:
        peers, length = (lax.axis_size(axis), shard.shape[dim])
        up = [(i, (i + 1) % peers) for i in range(peers)]
        down = [(j, i) for i, j in up]
        last = lax.slice_in_dim(shard, length - width, length, axis=dim)
        leading = lax.slice_in_dim(shard, 0, width, axis=dim)
        before = lax.ppermute(last, axis, up)
        after = lax.ppermute(leading, axis, down)
        shard = jnp.concatenate([before, shard, after], axis=dim)
    return shard


def interface_solve(first_row, last_row, top_left, top_right, low_left, low_right, link_rates):
    band_count = link_rates.shape[1]
    crossings = band_count - 1
    nothing = jnp.zeros_like(first_row[:, 0])
    flat_zero = jnp.zeros_like(link_rates[:, :1])
    carry_base = nothing
    carry_slope = flat_zero
    records = []
    for crossing in range(crossings):
        if crossing > 0:
            back_link = (link_rates[:, crossing - 1] * low_left[:, crossing])[:, None]
        else:
            back_link = flat_zero
        self_link = (link_rates[:, crossing] * low_right[:, crossing])[:, None]
        fore_link = (link_rates[:, crossing] * top_left[:, crossing + 1])[:, None]
        if crossing + 1 < crossings:
            next_link = (link_rates[:, crossing + 1] * top_right[:, crossing + 1])[:, None]
        else:
            next_link = flat_zero
        steepness = back_link * carry_slope + self_link
        offset = last_row[:, crossing] + back_link * carry_base
        denominator = 1.0 - fore_link * steepness
        upper_base = (first_row[:, crossing + 1] + fore_link * offset) / denominator
        upper_slope = next_link / denominator
        carry_base = offset + steepness * upper_base
        carry_slope = steepness * upper_slope
        records.append((carry_base, carry_slope, upper_base, upper_slope))
    lower_values = [nothing] * crossings
    upper_values = [nothing] * crossings
    follow = nothing
    for crossing in reversed(range(crossings)):
        carry_base, carry_slope, upper_base, upper_slope = records[crossing]
        lower_values[crossing] = carry_base + carry_slope * follow
        upper_values[crossing] = upper_base + upper_slope * follow
        follow = upper_values[crossing]
    before = jnp.stack([nothing] + lower_values, axis=1)
    beyond = jnp.stack(upper_values + [nothing], axis=1)
    return (before, beyond)


def per_device(fields, velocity, shifts, block_inverse, coupling):
    shard_cells = fields.shape[3]
    shard_hops = shifts // shard_cells
    remainder = shifts - shard_hops * shard_cells
    moving = fields
    sections = (lax.axis_size("az") - 1).bit_length()
    for section in range(sections):
        arrived = shifted(moving, "az", 1 << section)
        chosen = (shard_hops >> section) % 2 == 1
        moving = jnp.where(chosen[None, None, :, None], arrived, moving)
    previous = shifted(moving, "az", 1)
    joined = jnp.concatenate([previous, moving], axis=3)
    rotated = jax.vmap(
        lambda one_row, opening: lax.dynamic_slice_in_dim(one_row, opening, shard_cells, axis=-1),
        in_axes=(2, 0),
        out_axes=2,
    )(joined, shard_cells - remainder)
    stacked = jnp.concatenate([rotated, velocity[None]], axis=0)
    padded = extended(stacked, (("az", 3),), 1)
    values = padded[:5]
    speed = padded[5:]
    outflow = (
        jnp.maximum(speed[..., :-1], 0.0) * values[..., :-1]
        + jnp.minimum(speed[..., :-1], 0.0) * values[..., 1:]
    )
    transported = values[..., 1:-1] - (outflow[..., 1:] - outflow[..., :-1])
    energy = transported[4]
    local_part = jnp.einsum("zrl,zlp->zrp", block_inverse, energy, precision=lax.Precision.HIGHEST)
    corners = jnp.stack(
        [
            block_inverse[:, 0, 0],
            block_inverse[:, 0, -1],
            block_inverse[:, -1, 0],
            block_inverse[:, -1, -1],
        ],
        axis=1,
    )[:, None, :]
    first_all, last_all, corner_all, link_all = (
        lax.all_gather(local_part[:, :1, :], "rad", axis=1, tiled=True),
        lax.all_gather(local_part[:, -1:, :], "rad", axis=1, tiled=True),
        lax.all_gather(corners, "rad", axis=1, tiled=True),
        lax.all_gather(coupling, "rad", axis=1, tiled=True),
    )
    before, beyond = interface_solve(
        first_all,
        last_all,
        corner_all[..., 0],
        corner_all[..., 1],
        corner_all[..., 2],
        corner_all[..., 3],
        link_all,
    )
    band_index = lax.axis_index("rad")
    before_own = lax.dynamic_index_in_dim(before, band_index, 1, keepdims=False)
    beyond_own = lax.dynamic_index_in_dim(beyond, band_index, 1, keepdims=False)
    link_prev = jnp.concatenate([jnp.zeros_like(link_all[:, :1]), link_all[:, :-1]], axis=1)
    prev_own = lax.dynamic_index_in_dim(link_prev, band_index, 1, keepdims=False)
    link_own = coupling[:, 0]
    diffused = (
        local_part
        + (prev_own[:, None] * block_inverse[:, :, 0])[:, :, None] * before_own[:, None, :]
        + (link_own[:, None] * block_inverse[:, :, -1])[:, :, None] * beyond_own[:, None, :]
    )
    return jnp.concatenate([transported[:4], diffused[None]], axis=0)


def solution(mesh):
    placed = (
        P(None, None, "rad", "az"),
        P(None, "rad", "az"),
        P("rad"),
        P(None, "rad", None),
        P(None, "rad"),
    )
    return jax.shard_map(
        per_device,
        mesh=mesh,
        in_specs=placed,
        out_specs=P(None, None, "rad", "az"),
        check_vma=False,
    )
```

profile of v0, /device:TPU:0, one launch (start us, length us, event | category | flops | bytes accessed | tf_op | source)
XLA Modules:
  0.0 436.5 jit_solution(17480261281971726092)
XLA Ops:
  0.0 0.7 fusion.23
  0.7 25.5 %collective-permute-done = f32[5,8,64,128]{3,2,1,0:T(8,128)S(1)} collective-permute-done((f32[5,8,64,128]{3,2,1,0:T(8,128)}, f32[5,8,64,128]{3,2,1,0:T(8,128)S(1)}, u32[]{:S(2)}, u32[]{:S(2)}) %collective-permute-start) | collective-permute-done | bytes 1310752 | tf_op jit(solution)/shard_map/ppermute | solution.py:10
  26.2 1.6 broadcast_select_fusion
  27.9 38.1 %collective-permute-done.1 = f32[5,8,64,128]{3,2,1,0:T(8,128)S(1)} collective-permute-done((f32[5,8,64,128]{3,2,1,0:T(8,128)S(1)}, f32[5,8,64,128]{3,2,1,0:T(8,128)S(1)}, u32[]{:S(2)}, u32[]{:S(2)}) %collective-permute-start.1) | collective-permute-done | bytes 1310752 | tf_op jit(solution)/shard_map/ppermute | solution.py:10
  66.3 40.9 %collective-permute-start.2 = (f32[5,8,64,128]{3,2,1,0:T(8,128)S(1)}, f32[5,8,64,128]{3,2,1,0:T(8,128)S(1)}, u32[]{:S(2)}, u32[]{:S(2)}) collective-permute-start(f32[5,8,64,128]{3,2,1,0:T(8,128)S(1)} %broadcast_select_fusion.1), channel_id=1, source_target_pairs={{224,0},{232,8},{240,16},{248,24},{0,32},{8,40},{16,48},{24,56},{3... | collective-permute-start | bytes 3932168 | tf_op jit(solution)/shard_map/ppermute | solution.py:10
  107.1 32.1 %collective-permute-done.2 = f32[5,8,64,128]{3,2,1,0:T(8,128)S(1)} collective-permute-done((f32[5,8,64,128]{3,2,1,0:T(8,128)S(1)}, f32[5,8,64,128]{3,2,1,0:T(8,128)S(1)}, u32[]{:S(2)}, u32[]{:S(2)}) %collective-permute-start.2) | collective-permute-done | bytes 1310752 | tf_op jit(solution)/shard_map/ppermute | solution.py:10
  139.7 40.0 %collective-permute-done.3 = f32[5,8,64,128]{3,2,1,0:T(8,128)S(1)} collective-permute-done((f32[5,8,64,128]{3,2,1,0:T(8,128)S(1)}, f32[5,8,64,128]{3,2,1,0:T(8,128)S(1)}, u32[]{:S(2)}, u32[]{:S(2)}) %collective-permute-start.3) | collective-permute-done | bytes 1310752 | tf_op jit(solution)/shard_map/ppermute | solution.py:10
  180.0 0.6 copy-done
  181.0 30.1 %all-gather.1 = f32[8,1,8]{2,1,0:T(1,128)S(1)} all-gather(f32[1,1,8]{2,1,0:T(1,128)S(1)} %bitcast.199), channel_id=1, replica_groups=mesh['az'=32,'rad'=8] {'rad'}, dimensions={0}, use_global_device_ids=true | all-gather | bytes 288 | tf_op jit(solution)/shard_map/all_gather | solution.py:107
  211.3 23.7 %all-gather.2 = f32[8,4,8]{2,1,0:T(4,128)S(1)} all-gather(f32[1,4,8]{2,1,0:T(4,128)S(1)} %maximum_bitcast_fusion.1), channel_id=2, replica_groups=mesh['az'=32,'rad'=8] {'rad'}, dimensions={0}, use_global_device_ids=true | all-gather | bytes 1152 | tf_op jit(solution)/shard_map/all_gather | solution.py:106
  235.0 0.6 multiply_bitcast_fusion.2
  235.7 0.5 multiply_bitcast_fusion.3
  236.2 0.5 multiply_bitcast_fusion.6
  237.7 0.6 fusion.31
  238.3 0.6 fusion.37
  239.0 0.6 fusion.24
  239.6 32.1 %collective-permute-done.5 = f32[5,8,64,128]{3,2,1,0:T(8,128)S(1)} collective-permute-done((f32[5,8,64,128]{3,2,1,0:T(8,128)S(1)}, f32[5,8,64,128]{3,2,1,0:T(8,128)S(1)}, u32[]{:S(2)}, u32[]{:S(2)}) %collective-permute-start.5) | collective-permute-done | bytes 1310752 | tf_op jit(solution)/shard_map/ppermute | solution.py:10
  271.9 48.9 %copy.70 = f32[5,8,64,256]{1,0,2,3:T(8,128)} copy(f32[5,8,64,256]{3,2,1,0:T(8,128)S(1)} %pad_maximum_fusion.4) | data formatting | bytes 5242880 | tf_op jit(solution)/shard_map/concatenate | solution.py:77
  320.8 24.3 %gather_fusion = f32[64,5,8,128]{2,1,3,0:T(8,128)} fusion(f32[64,5,8,256]{2,1,0,3:T(8,128)} %bitcast, s32[64]{0:T(128)S(1)} %get-tuple-element.40), kind=kCustom, calls=%fused_computation | custom fusion | bytes 2622464 | tf_op jit(solution)/shard_map/vmap()/gather | solution.py:79
  345.1 13.7 %copy.71 = f32[64,5,8,128]{3,0,2,1:T(8,128)S(1)} copy(f32[64,5,8,128]{2,1,3,0:T(8,128)} %gather_fusion) | data formatting | bytes 2621440 | tf_op jit(solution)/shard_map/vmap()/gather | solution.py:79
  358.9 1.8 slice_maximum_fusion
  360.6 1.9 copy.72
  362.8 0.6 constant_dynamic-update-slice_fusion.7
  363.9 6.0 %collective-permute-start.7 = (f32[6,8,64,1]{2,1,3,0:T(8,128)S(1)}, f32[6,8,64,1]{2,1,3,0:T(8,128)S(1)}, u32[]{:S(2)}, u32[]{:S(2)}) collective-permute-start(f32[6,8,64,1]{2,1,3,0:T(8,128)S(1)} %copy.74), channel_id=1, source_target_pairs={{8,0},{16,8},{24,16},{32,24},{40,32},{48,40},{56,48},{64,56},{72,6... | collective-permute-start | bytes 36872 | tf_op jit(solution)/shard_map/ppermute | solution.py:21
  370.3 0.5 copy.73
  370.8 1.0 maximum_bitcast_fusion
  371.8 0.8 minimum_bitcast_fusion
  372.7 1.7 copy.75
  374.4 2.3 fusion.1
  378.0 28.1 %all_gather.13 = f32[8,8,128]{2,0,1:T(8,128)S(1)} all-gather(f32[8,1,128]{2,0,1:T(8,128)S(1)} %bitcast.178), channel_id=1, replica_groups=mesh['az'=32,'rad'=8] {'rad'}, dimensions={1}, use_global_device_ids=true | all-gather | bytes 36864 | tf_op jit(solution)/shard_map/all_gather | solution.py:105
  406.1 28.0 %all_gather.15 = f32[8,8,128]{2,0,1:T(8,128)S(1)} all-gather(f32[8,1,128]{2,0,1:T(8,128)S(1)} %bitcast.177), channel_id=1, replica_groups=mesh['az'=32,'rad'=8] {'rad'}, dimensions={1}, use_global_device_ids=true | all-gather | bytes 36864 | tf_op jit(solution)/shard_map/all_gather | solution.py:104
  435.4 1.1 pad_maximum_fusion.6
  (128 shorter events, 6.1 us)
Async XLA Ops:
  0.0 26.2 %collective-permute-start = (f32[5,8,64,128]{3,2,1,0:T(8,128)}, f32[5,8,64,128]{3,2,1,0:T(8,128)S(1)}, u32[]{:S(2)}, u32[]{:S(2)}) collective-permute-start(f32[5,8,64,128]{3,2,1,0:T(8,128)} %param.5), channel_id=1, source_target_pairs={{248,0},{0,8},{8,16},{16,24},{24,32},{32,40},{40,48},{48,56},{56,6... | collective-permute-start | bytes 3932168 | tf_op jit(solution)/shard_map/ppermute | solution.py:10
  27.8 38.1 %collective-permute-start.1 = (f32[5,8,64,128]{3,2,1,0:T(8,128)S(1)}, f32[5,8,64,128]{3,2,1,0:T(8,128)S(1)}, u32[]{:S(2)}, u32[]{:S(2)}) collective-permute-start(f32[5,8,64,128]{3,2,1,0:T(8,128)S(1)} %broadcast_select_fusion), channel_id=1, source_target_pairs={{240,0},{248,8},{0,16},{8,24},{16,32},{24,40},{32,48},{40,56},{48,... | collective-permute-start | bytes 3932168 | tf_op jit(solution)/shard_map/ppermute | solution.py:10
  66.3 73.0 %collective-permute-start.2 = (f32[5,8,64,128]{3,2,1,0:T(8,128)S(1)}, f32[5,8,64,128]{3,2,1,0:T(8,128)S(1)}, u32[]{:S(2)}, u32[]{:S(2)}) collective-permute-start(f32[5,8,64,128]{3,2,1,0:T(8,128)S(1)} %broadcast_select_fusion.1), channel_id=1, source_target_pairs={{224,0},{232,8},{240,16},{248,24},{0,32},{8,40},{16,48},{24,56},{3... | collective-permute-start | bytes 3932168 | tf_op jit(solution)/shard_map/ppermute | solution.py:10
  139.6 40.1 %collective-permute-start.3 = (f32[5,8,64,128]{3,2,1,0:T(8,128)S(1)}, f32[5,8,64,128]{3,2,1,0:T(8,128)S(1)}, u32[]{:S(2)}, u32[]{:S(2)}) collective-permute-start(f32[5,8,64,128]{3,2,1,0:T(8,128)S(1)} %broadcast_select_fusion.2), channel_id=1, source_target_pairs={{192,0},{200,8},{208,16},{216,24},{224,32},{232,40},{240,48},{248,... | collective-permute-start | bytes 3932168 | tf_op jit(solution)/shard_map/ppermute | solution.py:10
  179.9 56.8 %collective-permute-start.4 = (f32[5,8,64,128]{3,2,1,0:T(8,128)S(1)}, f32[5,8,64,128]{3,2,1,0:T(8,128)S(1)}, u32[]{:S(2)}, u32[]{:S(2)}) collective-permute-start(f32[5,8,64,128]{3,2,1,0:T(8,128)S(1)} %broadcast_select_fusion.3), channel_id=1, source_target_pairs={{128,0},{136,8},{144,16},{152,24},{160,32},{168,40},{176,48},{184,... | collective-permute-start | bytes 3932168 | tf_op jit(solution)/shard_map/ppermute | solution.py:10
  237.0 34.7 %collective-permute-start.5 = (f32[5,8,64,128]{3,2,1,0:T(8,128)S(1)}, f32[5,8,64,128]{3,2,1,0:T(8,128)S(1)}, u32[]{:S(2)}, u32[]{:S(2)}) collective-permute-start(f32[5,8,64,128]{3,2,1,0:T(8,128)S(1)} %broadcast_select_fusion.4), channel_id=1, source_target_pairs={{248,0},{0,8},{8,16},{16,24},{24,32},{32,40},{40,48},{48,56},{56,6... | collective-permute-start | bytes 3932168 | tf_op jit(solution)/shard_map/ppermute | solution.py:10
  362.6 7.7 %collective-permute-start.6 = (f32[6,8,64,1]{2,1,3,0:T(8,128)S(1)}, f32[6,8,64,1]{2,1,3,0:T(8,128)S(1)}, u32[]{:S(2)}, u32[]{:S(2)}) collective-permute-start(f32[6,8,64,1]{2,1,3,0:T(8,128)S(1)} %copy.72), channel_id=1, source_target_pairs={{0,8},{8,16},{16,24},{24,32},{32,40},{40,48},{48,56},{56,64},{64,7... | collective-permute-start | bytes 36872 | tf_op jit(solution)/shard_map/ppermute | solution.py:20
  363.9 8.7 %collective-permute-start.7 = (f32[6,8,64,1]{2,1,3,0:T(8,128)S(1)}, f32[6,8,64,1]{2,1,3,0:T(8,128)S(1)}, u32[]{:S(2)}, u32[]{:S(2)}) collective-permute-start(f32[6,8,64,1]{2,1,3,0:T(8,128)S(1)} %copy.74), channel_id=1, source_target_pairs={{8,0},{16,8},{24,16},{32,24},{40,32},{48,40},{56,48},{64,56},{72,6... | collective-permute-start | bytes 36872 | tf_op jit(solution)/shard_map/ppermute | solution.py:21
  377.6 56.6 %copy-start.3 = (f32[8,1]{0,1:T(1,128)S(1)}, f32[8,1]{0,1:T(1,128)}, u32[]{:S(2)}) copy-start(f32[8,1]{0,1:T(1,128)} %copy-done.2) | copy-start | bytes 100
  377.6 56.5 %copy-start.5 = (f32[8,1]{0,1:T(1,128)S(1)}, f32[8,1]{0,1:T(1,128)}, u32[]{:S(2)}) copy-start(f32[8,1]{0,1:T(1,128)} %copy-done.4) | copy-start | bytes 100
  377.6 56.5 %copy-start.7 = (f32[8,1]{0,1:T(1,128)S(1)}, f32[8,1]{0,1:T(1,128)}, u32[]{:S(2)}) copy-start(f32[8,1]{0,1:T(1,128)} %copy-done.6) | copy-start | bytes 100
  377.6 56.5 %copy-start.8 = (f32[8]{0:T(128)S(1)}, f32[8]{0:T(128)}, u32[]{:S(2)}) copy-start(f32[8]{0:T(128)} %get-tuple-element.53) | copy-start | bytes 100
  377.6 56.5 %copy-start.9 = (f32[8]{0:T(128)S(1)}, f32[8]{0:T(128)}, u32[]{:S(2)}) copy-start(f32[8]{0:T(128)} %get-tuple-element.63) | copy-start | bytes 100
  377.7 56.5 %copy-start.10 = (f32[8]{0:T(128)S(1)}, f32[8]{0:T(128)}, u32[]{:S(2)}) copy-start(f32[8]{0:T(128)} %get-tuple-element.55) | copy-start | bytes 100
  377.7 56.5 %copy-start.11 = (f32[8]{0:T(128)S(1)}, f32[8]{0:T(128)}, u32[]{:S(2)}) copy-start(f32[8]{0:T(128)} %get-tuple-element.64) | copy-start | bytes 100
  377.7 56.5 %copy-start.12 = (f32[8]{0:T(128)S(1)}, f32[8]{0:T(128)}, u32[]{:S(2)}) copy-start(f32[8]{0:T(128)} %get-tuple-element.57) | copy-start | bytes 100
  377.7 56.5 %copy-start.13 = (f32[8]{0:T(128)S(1)}, f32[8]{0:T(128)}, u32[]{:S(2)}) copy-start(f32[8]{0:T(128)} %get-tuple-element.65) | copy-start | bytes 100
  377.7 56.5 %copy-start.15 = (f32[8,1]{0,1:T(1,128)S(1)}, f32[8,1]{0,1:T(1,128)}, u32[]{:S(2)}) copy-start(f32[8,1]{0,1:T(1,128)} %copy-done.14) | copy-start | bytes 100
  377.7 56.5 %copy-start.17 = (f32[8,1]{0,1:T(1,128)S(1)}, f32[8,1]{0,1:T(1,128)}, u32[]{:S(2)}) copy-start(f32[8,1]{0,1:T(1,128)} %copy-done.16) | copy-start | bytes 100
  377.7 56.5 %copy-start.23 = (f32[8,1]{0,1:T(1,128)S(1)}, f32[8,1]{0,1:T(1,128)}, u32[]{:S(2)}) copy-start(f32[8,1]{0,1:T(1,128)} %copy-done.22) | copy-start | bytes 100
  377.7 56.5 %copy-start.24 = (f32[8]{0:T(128)S(1)}, f32[8]{0:T(128)}, u32[]{:S(2)}) copy-start(f32[8]{0:T(128)} %get-tuple-element.66) | copy-start | bytes 100
  377.7 56.5 %copy-start.25 = (f32[8]{0:T(128)S(1)}, f32[8]{0:T(128)}, u32[]{:S(2)}) copy-start(f32[8]{0:T(128)} %get-tuple-element.67) | copy-start | bytes 100
  377.7 56.5 %copy-start.26 = (f32[8]{0:T(128)S(1)}, f32[8]{0:T(128)}, u32[]{:S(2)}) copy-start(f32[8]{0:T(128)} %get-tuple-element.68) | copy-start | bytes 100
  377.8 56.5 %copy-start.27 = (f32[8]{0:T(128)S(1)}, f32[8]{0:T(128)}, u32[]{:S(2)}) copy-start(f32[8]{0:T(128)} %get-tuple-element.69) | copy-start | bytes 100
  377.8 56.7 %copy-start.19 = (f32[8,1]{0,1:T(1,128)S(1)}, f32[8,1]{0,1:T(1,128)}, u32[]{:S(2)}) copy-start(f32[8,1]{0,1:T(1,128)} %copy-done.18) | copy-start | bytes 100
  377.9 56.8 %copy-start.42 = (f32[8]{0:T(128)S(1)}, f32[8]{0:T(128)}, u32[]{:S(2)}) copy-start(f32[8]{0:T(128)} %multiply_bitcast_fusion.8) | copy-start | bytes 100
  377.9 56.9 %copy-start.40 = (f32[8]{0:T(128)S(1)}, f32[8]{0:T(128)}, u32[]{:S(2)}) copy-start(f32[8]{0:T(128)} %get-tuple-element.92) | copy-start | bytes 100
  377.9 56.9 %copy-start.39 = (f32[8]{0:T(128)S(1)}, f32[8]{0:T(128)}, u32[]{:S(2)}) copy-start(f32[8]{0:T(128)} %get-tuple-element.91) | copy-start | bytes 100
  377.9 57.0 %copy-start.37 = (f32[8]{0:T(128)S(1)}, f32[8]{0:T(128)}, u32[]{:S(2)}) copy-start(f32[8]{0:T(128)} %get-tuple-element.82) | copy-start | bytes 100
  377.9 57.1 %copy-start.36 = (f32[8]{0:T(128)S(1)}, f32[8]{0:T(128)}, u32[]{:S(2)}) copy-start(f32[8]{0:T(128)} %get-tuple-element.90) | copy-start | bytes 100
  377.9 57.1 %copy-start.21 = (f32[8,1]{0,1:T(1,128)S(1)}, f32[8,1]{0,1:T(1,128)}, u32[]{:S(2)}) copy-start(f32[8,1]{0,1:T(1,128)} %copy-done.20) | copy-start | bytes 100
  377.9 57.1 %copy-start.41 = (f32[8]{0:T(128)S(1)}, f32[8]{0:T(128)}, u32[]{:S(2)}) copy-start(f32[8]{0:T(128)} %get-tuple-element.9) | copy-start | bytes 100
  (19 other events, 486.3 us)
where the time goes:
time: 437 us
  waiting for transfers between devices  168 us (38%)
  blocking collectives  110 us (25%)
  local copies, waits for them, and re-layouts  93.7 us (21%)
  starting transfers between devices  47.4 us (11%)
  other arithmetic  16.2 us (4%)
    ppermute x6, waiting for transfers between devices, shifted(): return lax.ppermute(block, axis, route)  168 us
    concatenate x1, local copies, waits for them, and re-layouts, per_device(): joined = jnp.concatenate([previous, moving], axis=3)  48.9 us
    ppermute x6, starting transfers between devices, shifted(): return lax.ppermute(block, axis, route)  41.2 us
    gather x2, local copies, waits for them, and re-layouts, per_device(): lax.dynamic_slice_in_dim(one_row, opening, shard_cells, axis=-1)  38 us
    all_gather x1, blocking collectives, per_device(): lax.all_gather(coupling, 'rad', axis=1, tiled=True)  30.1 us
    all_gather x1, blocking collectives, per_device(): lax.all_gather(local_part[:, -1:, :], 'rad', axis=1, tiled=True)  28.1 us
    all_gather x1, blocking collectives, per_device(): lax.all_gather(local_part[:, :1, :], 'rad', axis=1, tiled=True)  28 us
    all_gather x1, blocking collectives, per_device(): lax.all_gather(corners, 'rad', axis=1, tiled=True)  23.7 us
  transfers between devices with their start and end apart: 8, of which 6 were waited for; matrix products, arithmetic and copies ran while one was open for 2% of the time, Pallas kernels for 0%

commit v1 on v0

v1 whole, which is shorter than its diff:
```python
import functools

import jax
import jax.numpy as jnp
from jax import lax
from jax.experimental import pallas as pl
from jax.experimental.pallas import tpu as pltpu
from jax.sharding import PartitionSpec as P

MESH = pl.DeviceIdType.MESH
LANES = 128
F32 = jnp.float32


def lane_index():
    return lax.broadcasted_iota(jnp.int32, (8, LANES), 1)


def kernel(az, rad, nf, rows, *refs):
    nth = 8
    own = rows // az
    order = [nf - 1] + list(range(nf - 1))
    (f_hbm, v_hbm, shifts_hbm, g_hbm, link_hbm, out) = refs[:6]
    (raw, raw_v, g, staged, turned, arrived, speed, energy, local) = refs[6:15]
    (edge, edge_in, speed_edge, speed_edge_in) = refs[15:19]
    (corner, corner_in, ends, ends_in, joined) = refs[19:24]
    (shifts, link) = refs[24:26]
    (in_sem, par_sem, send_a, recv_a, send_b, recv_b, send_e, recv_e, send_r, recv_r) = refs[26:36]
    homes = refs[36 : 36 + nf]

    me = lax.axis_index("az")
    band = lax.axis_index("rad")
    right = lax.rem(me + 1, az)
    left = lax.rem(me + az - 1, az)
    lane = lane_index()

    loads = [pltpu.make_async_copy(f_hbm.at[f], raw.at[i], in_sem.at[i]) for i, f in enumerate(order)]
    params = [
        pltpu.make_async_copy(v_hbm, raw_v, par_sem.at[0]),
        pltpu.make_async_copy(g_hbm, g, par_sem.at[1]),
        pltpu.make_async_copy(shifts_hbm, shifts, par_sem.at[2]),
        pltpu.make_async_copy(link_hbm, link, par_sem.at[3]),
    ]
    for copy in loads[:1] + params + loads[1:]:
        copy.start()

    barrier = pltpu.get_barrier_semaphore()

    def greet_az(k, carry):
        pl.semaphore_signal(barrier, 1, device_id={"az": lax.rem(me + k, az), "rad": band}, device_id_type=MESH)
        return carry

    def greet_rad(k, carry):
        pl.semaphore_signal(barrier, 1, device_id={"az": me, "rad": lax.rem(band + k, rad)}, device_id_type=MESH)
        return carry

    lax.fori_loop(1, az, greet_az, 0)
    lax.fori_loop(1, rad, greet_rad, 0)

    def stage(i):
        loads[i].wait()

        def row(r, carry):
            staged[i, r] = raw[i, pl.ds(r, nth, stride=rows), :]
            return carry

        lax.fori_loop(0, rows, row, 0, unroll=8)

    def send_out(i):
        def to(k, carry):
            m = lax.rem(me + k, az)
            pltpu.make_async_remote_copy(
                staged.at[i, pl.ds(m * own, own)],
                homes[i].at[me],
                send_a.at[i],
                recv_a.at[i],
                device_id={"az": m, "rad": band},
                device_id_type=MESH,
            ).start()
            return carry

        lax.fori_loop(1, az, to, 0)
        homes[i][me] = staged[i, pl.ds(me * own, own)]

    def wait_bytes(ref, sem):
        pltpu.make_async_copy(ref, ref, sem).wait()

    def rotate(i):
        wait_bytes(homes[i].at[pl.ds(0, az - 1)], recv_a.at[i])
        for j in range(own):
            shift = shifts[me * own + j]
            hops = lax.shift_right_logical(shift, 7)
            rest = jnp.bitwise_and(shift, LANES - 1)
            carried = lane >= rest

            def block(b, previous, j=j, hops=hops, rest=rest, carried=carried):
                origin = jnp.bitwise_and(b - hops, az - 1)
                current = pltpu.roll(homes[i][origin, j], rest, 1)
                turned[i, b, j] = jnp.where(carried, current, previous)
                return current

            opening = pltpu.roll(homes[i][jnp.bitwise_and(az - 1 - hops, az - 1), j], rest, 1)
            lax.fori_loop(0, az, block, opening, unroll=8)

    def send_home(i):
        def to(k, carry):
            m = lax.rem(me + k, az)
            pltpu.make_async_remote_copy(
                turned.at[i, m],
                arrived.at[i, pl.ds(me * own, own)],
                send_b.at[i],
                recv_b.at[i],
                device_id={"az": m, "rad": band},
                device_id_type=MESH,
            ).start()
            return carry

        lax.fori_loop(1, az, to, 0)
        arrived[i, pl.ds(me * own, own)] = turned[i, me]

    key = jnp.bitwise_and(lax.shift_right_logical(lane + 1, 1), LANES // 2 - 1)

    def packed(load):
        def row(r, carry):
            return jnp.where(key == r, pltpu.roll(load(r), 2 * r, 1), carry)

        return lax.fori_loop(0, rows, row, jnp.zeros((8, LANES), F32), unroll=8)

    def edge_copies(i):
        return [
            pltpu.make_async_remote_copy(
                edge.at[i],
                edge_in.at[i, side],
                send_e.at[i],
                recv_e.at[i],
                device_id={"az": to, "rad": band},
                device_id_type=MESH,
            )
            for side, to in enumerate((right, left))
        ]

    def send_edges(i):
        wait_bytes(arrived.at[i, pl.ds(0, rows - own)], recv_b.at[i])
        edge[i] = packed(lambda r: arrived[i, r])
        for copy in edge_copies(i):
            copy.start()

    def speed_copy():
        return pltpu.make_async_remote_copy(
            speed_edge,
            speed_edge_in,
            send_e.at[nf],
            recv_e.at[nf],
            device_id={"az": right, "rad": band},
            device_id_type=MESH,
        )

    def to_bands(source, target, which, start):
        def to(k, carry):
            copy = pltpu.make_async_remote_copy(
                source,
                target.at[band],
                send_r.at[which],
                recv_r.at[which],
                device_id={"az": me, "rad": lax.rem(band + k, rad)},
                device_id_type=MESH,
            )
            copy.start()
            return carry

        lax.fori_loop(1, rad, to, 0)

    def advect(i):
        wait_bytes(edge_in.at[i], recv_e.at[i])
        own_edge = edge[i]
        from_left = pltpu.roll(edge_in[i, 0], 2, 1)
        from_right = edge_in[i, 1]
        speed_left = pltpu.roll(speed_edge_in[...], 2, 1)
        first = pltpu.roll(own_edge, 1, 1)
        entering = jnp.maximum(speed_left, 0.0) * from_left + jnp.minimum(speed_left, 0.0) * first
        sides = jnp.where(jnp.bitwise_and(lane, 1) == 1, entering, from_right)

        def row(r, carry):
            side = pltpu.roll(sides, LANES - 1 - 2 * r, 1)
            value = arrived[i, r]
            rate = speed[r]
            ahead = jnp.where(lane == LANES - 1, side, pltpu.roll(value, LANES - 1, 1))
            outflow = jnp.maximum(rate, 0.0) * value + jnp.minimum(rate, 0.0) * ahead
            inflow = jnp.where(lane == 0, side, pltpu.roll(outflow, 1, 1))
            moved = value - (outflow - inflow)
            if i == 0:
                energy[pl.ds(r, nth, stride=rows), :] = moved
            else:
                out[order[i], pl.ds(r, nth, stride=rows), :] = moved
            return carry

        lax.fori_loop(0, rows, row, 0, unroll=8)

    def solve_local():
        for z in range(nth):
            part = jnp.dot(
                g[z],
                energy[z * rows : (z + 1) * rows, :],
                precision=lax.Precision.HIGHEST,
                preferred_element_type=F32,
            )
            local[z] = part
            ends[0, z : z + 1, :] = part[:1]
            ends[1, z : z + 1, :] = part[rows - 1 :]
        ends_in[band] = ends[...]
        to_bands(ends, ends_in, 1, True)

    def interface():
        wait_bytes(corner_in.at[pl.ds(0, rad - 1)], recv_r.at[0])
        wait_bytes(ends_in.at[pl.ds(0, rad - 1)], recv_r.at[1])
        top_left, top_right, low_left, low_right, rates = (
            [corner_in[k][:, c : c + 1] for k in range(rad)] for c in range(5)
        )
        crossings = rad - 1
        zero = jnp.zeros((8, 1), F32)
        nothing = jnp.zeros((8, LANES), F32)
        base, slope = nothing, zero
        records = []
        for k in range(crossings):
            back = rates[k - 1] * low_left[k] if k > 0 else zero
            here = rates[k] * low_right[k]
            fore = rates[k] * top_left[k + 1]
            onward = rates[k + 1] * top_right[k + 1] if k + 1 < crossings else zero
            steep = back * slope + here
            offset = ends_in[k, 1] + back * base
            scale = 1.0 - fore * steep
            upper_base = (ends_in[k + 1, 0] + fore * offset) / scale
            upper_slope = onward / scale
            base = offset + steep * upper_base
            slope = steep * upper_slope
            records.append((base, slope, upper_base, upper_slope))
        follow = nothing
        joined[0, 0] = nothing
        joined[rad - 1, 1] = nothing
        for k in reversed(range(crossings)):
            base, slope, upper_base, upper_slope = records[k]
            joined[k + 1, 0] = rates[k] * (base + slope * follow)
            follow = upper_base + upper_slope * follow
            joined[k, 1] = rates[k] * follow
        before = joined[band, 0]
        beyond = joined[band, 1]
        for z in range(nth):
            block = g[z]
            out[nf - 1, z * rows : (z + 1) * rows, :] = (
                local[z] + block[:, :1] * before[z : z + 1] + block[:, rows - 1 :] * beyond[z : z + 1]
            )

    def prepare():
        for copy in params:
            copy.wait()

        def row(r, carry):
            speed[r] = raw_v[pl.ds(r, nth, stride=rows), :]
            return carry

        lax.fori_loop(0, rows, row, 0, unroll=8)
        speed_edge[...] = packed(lambda r: speed[r])
        speed_copy().start()
        sub = lax.broadcasted_iota(jnp.int32, (8, LANES), 0)
        table = jnp.zeros((8, LANES), F32)
        for z in range(nth):
            block = g[z]
            entries = [block[0:1, 0:1], block[0:1, rows - 1 :], block[rows - 1 :, 0:1], block[rows - 1 :, rows - 1 :]]
            for c, entry in enumerate(entries):
                table = jnp.where((sub == z) & (lane == c), entry, table)
            table = jnp.where((sub == z) & (lane == 4), link[z], table)
        corner[...] = table
        corner_in[band] = table
        to_bands(corner, corner_in, 0, True)

    stage(0)
    pl.semaphore_wait(barrier, az - 1 + rad - 1)
    send_out(0)
    stage(1)
    send_out(1)
    prepare()
    for i in range(2, nf):
        stage(i)
    for i in range(nf):
        rotate(i)
        send_home(i)
        if i + 2 < nf:
            send_out(i + 2)
        if i == 2:
            wait_bytes(speed_edge_in, recv_e.at[nf])
            advect(0)
            solve_local()
        if i == 4:
            interface()
        if i > 2:
            advect(i - 2)
        if i >= 1:
            send_edges(i - 1)
    send_edges(nf - 1)
    advect(nf - 2)
    advect(nf - 1)

    for i in range(nf):
        wait_bytes(staged.at[i, pl.ds(0, rows - own)], send_a.at[i])
        wait_bytes(turned.at[i, pl.ds(0, az - 1)], send_b.at[i])
        wait_bytes(edge_in.at[i], send_e.at[i])
    wait_bytes(speed_edge, send_e.at[nf])
    wait_bytes(corner_in.at[pl.ds(0, rad - 1)], send_r.at[0])
    wait_bytes(ends_in.at[pl.ds(0, rad - 1)], send_r.at[1])


def per_device(az, rad, fields, velocity, shifts, block_inverse, coupling):
    nf, nth, rows, lanes = fields.shape
    own = rows // az
    whole = nth * rows
    hbm = pl.BlockSpec(memory_space=pltpu.MemorySpace.HBM)
    vmem = pl.BlockSpec(memory_space=pltpu.MemorySpace.VMEM)
    dma = pltpu.SemaphoreType.DMA
    out = pl.pallas_call(
        functools.partial(kernel, az, rad, nf, rows),
        out_shape=jax.ShapeDtypeStruct((nf, whole, lanes), F32),
        in_specs=[hbm] * 5,
        out_specs=vmem,
        scratch_shapes=[
            pltpu.VMEM((nf, whole, lanes), F32),
            pltpu.VMEM((whole, lanes), F32),
            pltpu.VMEM((nth, rows, rows), F32),
            pltpu.VMEM((nf, rows, nth, lanes), F32),
            pltpu.VMEM((nf, az, own, nth, lanes), F32),
            pltpu.VMEM((nf, rows, nth, lanes), F32),
            pltpu.VMEM((rows, nth, lanes), F32),
            pltpu.VMEM((whole, lanes), F32),
            pltpu.VMEM((nth, rows, lanes), F32),
            pltpu.VMEM((nf, nth, lanes), F32),
            pltpu.VMEM((nf, 2, nth, lanes), F32),
            pltpu.VMEM((nth, lanes), F32),
            pltpu.VMEM((nth, lanes), F32),
            pltpu.VMEM((nth, lanes), F32),
            pltpu.VMEM((rad, nth, lanes), F32),
            pltpu.VMEM((2, nth, lanes), F32),
            pltpu.VMEM((rad, 2, nth, lanes), F32),
            pltpu.VMEM((rad, 2, nth, lanes), F32),
            pltpu.SMEM((rows,), jnp.int32),
            pltpu.SMEM((nth,), F32),
            dma((nf,)),
            dma((4,)),
            dma((nf,)),
            dma((nf,)),
            dma((nf,)),
            dma((nf,)),
            dma((nf + 1,)),
            dma((nf + 1,)),
            dma((2,)),
            dma((2,)),
        ]
        + [pltpu.VMEM((az, own, nth, lanes), F32)] * nf,
        compiler_params=pltpu.CompilerParams(
            collective_id=0, has_side_effects=True, vmem_limit_bytes=40 << 20
        ),
    )(
        fields.reshape(nf, whole, lanes),
        velocity.reshape(whole, lanes),
        shifts,
        block_inverse,
        coupling.reshape(nth),
    )
    return out.reshape(fields.shape)


def solution(mesh):
    placed = (
        P(None, None, "rad", "az"),
        P(None, "rad", "az"),
        P("rad"),
        P(None, "rad", None),
        P(None, "rad"),
    )
    return jax.shard_map(
        functools.partial(per_device, mesh.shape["az"], mesh.shape["rad"]),
        mesh=mesh,
        in_specs=placed,
        out_specs=P(None, None, "rad", "az"),
        check_vma=False,
    )
```

time: 437 us -> 89.6 us (0.21)
  the two profiles are of different devices: /device:TPU:0 before, /device:TPU:1 now
where the time goes in v1:
time: 89.6 us; the launch traced here: 89.4 us
  Pallas kernels  83.8 us (94%)
  local copies, waits for them, and re-layouts  5.58 us (6%)
    pallas_call x1, Pallas kernels, per_device(): pl.pallas_call(functools.partial(kernel, az, rad, nf, rows), out_shape=ja...  83.8 us
    unnamed x11, local copies, waits for them, and re-layouts  5.58 us

profile of v1, /device:TPU:1, one launch (start us, length us, event | category | flops | bytes accessed | tf_op | source)
XLA Modules:
  0.0 89.4 jit_solution(11812628463109978779)
XLA Ops:
  0.0 0.0 copy-start
  0.0 1.3 %copy-done = f32[5,8,64,128]{3,2,1,0:T(8,128)S(1)} copy-done((f32[5,8,64,128]{3,2,1,0:T(8,128)S(1)}, f32[5,8,64,128]{3,2,1,0:T(8,128)}, u32[]{:S(2)}) %copy-start) | copy-done | bytes 1310744
  1.3 0.0 copy-start.1
  1.3 0.9 %copy-done.1 = f32[8,64,128]{2,1,0:T(8,128)S(1)} copy-done((f32[8,64,128]{2,1,0:T(8,128)S(1)}, f32[8,64,128]{2,1,0:T(8,128)}, u32[]{:S(2)}) %copy-start.1) | copy-done | bytes 262168
  2.3 0.0 copy-start.2
  2.3 0.9 %copy-done.2 = f32[8,64,64]{2,1,0:T(8,128)S(1)} copy-done((f32[8,64,64]{2,1,0:T(8,128)S(1)}, f32[8,64,64]{2,1,0:T(8,128)}, u32[]{:S(2)}) %copy-start.2) | copy-done | bytes 131096
  3.2 0.0 copy-start.3
  3.2 0.7 copy-done.3
  3.9 0.0 copy-start.4
  3.9 0.7 copy-done.4
  4.5 83.8 %shard_map.55 = f32[5,512,128]{2,1,0:T(8,128)S(1)} custom-call(f32[5,512,128]{2,1,0:T(8,128)S(1)} %bitcast.5, f32[512,128]{1,0:T(8,128)S(1)} %bitcast.6, s32[64]{0:T(128)S(1)} %copy-done.3, f32[8,64,64]{2,1,0:T(8,128)S(1)} %copy-done.2, f32[8]{0:T(128)S(1)} %bitcast.7), custom_call_target="tpu_custom_call" | custom-call | tf_op jit(solution)/shard_map/pallas_call | solution.py:319
  88.4 1.1 %copy.7 = f32[5,8,64,128]{3,2,1,0:T(8,128)} copy(f32[5,8,64,128]{3,2,1,0:T(8,128)S(1)} %bitcast.4) | data formatting | bytes 2621440
Async XLA Ops:
  0.0 1.3 %copy-start = (f32[5,8,64,128]{3,2,1,0:T(8,128)S(1)}, f32[5,8,64,128]{3,2,1,0:T(8,128)}, u32[]{:S(2)}) copy-start(f32[5,8,64,128]{3,2,1,0:T(8,128)} %param.5) | copy-start | bytes 3932164
  1.3 0.9 %copy-start.1 = (f32[8,64,128]{2,1,0:T(8,128)S(1)}, f32[8,64,128]{2,1,0:T(8,128)}, u32[]{:S(2)}) copy-start(f32[8,64,128]{2,1,0:T(8,128)} %param.6) | copy-start | bytes 786436
  2.3 0.9 %copy-start.2 = (f32[8,64,64]{2,1,0:T(8,128)S(1)}, f32[8,64,64]{2,1,0:T(8,128)}, u32[]{:S(2)}) copy-start(f32[8,64,64]{2,1,0:T(8,128)} %refs_3_.1) | copy-start | bytes 393220
  3.2 0.7 copy-start.3
  3.9 0.7 copy-start.4

commit v2 on v1

--- a/solution.py
+++ b/solution.py
@@ -20,13 +20,15 @@
     nth = 8
     own = rows // az
     order = [nf - 1] + list(range(nf - 1))
+    groups = [[0], list(range(1, nf - 1)), [nf - 1]]
+    nrims = len(groups)
     (f_hbm, v_hbm, shifts_hbm, g_hbm, link_hbm, out) = refs[:6]
     (raw, raw_v, g, staged, turned, arrived, speed, energy, local) = refs[6:15]
-    (edge, edge_in, speed_edge, speed_edge_in) = refs[15:19]
-    (corner, corner_in, ends, ends_in, joined) = refs[19:24]
-    (shifts, link) = refs[24:26]
-    (in_sem, par_sem, send_a, recv_a, send_b, recv_b, send_e, recv_e, send_r, recv_r) = refs[26:36]
-    homes = refs[36 : 36 + nf]
+    (rim, rim_in, speed_edge, speed_edge_in, speed_back) = refs[15:20]
+    (corner, corner_in, ends, ends_in, joined) = refs[20:25]
+    (shifts, link) = refs[25:27]
+    (in_sem, par_sem, send_a, recv_a, send_b, recv_b, send_e, recv_e, send_r, recv_r) = refs[27:37]
+    homes = refs[37 : 37 + nf]
 
     me = lax.axis_index("az")
     band = lax.axis_index("rad")
@@ -87,20 +89,32 @@
 
     def rotate(i):
         wait_bytes(homes[i].at[pl.ds(0, az - 1)], recv_a.at[i])
-        for j in range(own):
-            shift = shifts[me * own + j]
-            hops = lax.shift_right_logical(shift, 7)
-            rest = jnp.bitwise_and(shift, LANES - 1)
-            carried = lane >= rest
-
-            def block(b, previous, j=j, hops=hops, rest=rest, carried=carried):
-                origin = jnp.bitwise_and(b - hops, az - 1)
-                current = pltpu.roll(homes[i][origin, j], rest, 1)
-                turned[i, b, j] = jnp.where(carried, current, previous)
-                return current
-
-            opening = pltpu.roll(homes[i][jnp.bitwise_and(az - 1 - hops, az - 1), j], rest, 1)
-            lax.fori_loop(0, az, block, opening, unroll=8)
+        shift = [shifts[me * own + j] for j in range(own)]
+        hops = [lax.shift_right_logical(v, 7) for v in shift]
+        rest = [jnp.bitwise_and(v, LANES - 1) for v in shift]
+        carried = [lane >= v for v in rest]
+
+        def turn(b, j):
+            return pltpu.roll(homes[i][jnp.bitwise_and(b + az - hops[j], az - 1), j], rest[j], 1)
+
+        def block(b, carry):
+            ahead = jnp.bitwise_and(b + 1, az - 1)
+            behind = jnp.bitwise_and(b + az - 1, az - 1)
+            made = []
+            for j in range(own):
+                previous, lefts, rights = carry[j]
+                current = turn(b, j)
+                value = jnp.where(carried[j], current, previous)
+                turned[i, b, j] = value
+                lefts = jnp.where(lane == ahead, pltpu.roll(value, ahead + 1, 1), lefts)
+                rights = jnp.where(lane == behind, pltpu.roll(value, behind, 1), rights)
+                made.append((current, lefts, rights))
+            return tuple(made)
+
+        zero = jnp.zeros((8, LANES), F32)
+        opening = tuple((turn(az - 1, j), zero, zero) for j in range(own))
+        done = lax.fori_loop(0, az, block, opening, unroll=4)
+        return [tile for j in range(own) for tile in done[j][1:]]
 
     def send_home(i):
         def to(k, carry):
@@ -126,31 +140,38 @@
 
         return lax.fori_loop(0, rows, row, jnp.zeros((8, LANES), F32), unroll=8)
 
-    def edge_copies(i):
-        return [
+    def send_rims(n, tiles):
+        tiles = tiles + [jnp.zeros((8, LANES), F32)] * (LANES // 8 - len(tiles))
+        rows_out = jnp.transpose(jnp.concatenate(tiles, axis=0))
+        for b in range(az):
+            rim[n, b] = rows_out[b : b + 1]
+
+        def to(k, carry):
+            m = lax.rem(me + k, az)
             pltpu.make_async_remote_copy(
-                edge.at[i],
-                edge_in.at[i, side],
-                send_e.at[i],
-                recv_e.at[i],
-                device_id={"az": to, "rad": band},
+                rim.at[n, m],
+                rim_in.at[n, me],
+                send_e.at[n],
+                recv_e.at[n],
+                device_id={"az": m, "rad": band},
                 device_id_type=MESH,
-            )
-            for side, to in enumerate((right, left))
-        ]
-
-    def send_edges(i):
-        wait_bytes(arrived.at[i, pl.ds(0, rows - own)], recv_b.at[i])
-        edge[i] = packed(lambda r: arrived[i, r])
-        for copy in edge_copies(i):
-            copy.start()
+            ).start()
+            return carry
+
+        lax.fori_loop(1, az, to, 0)
+        rim_in[n, me] = rim[n, me]
+
+    def take_rims(n):
+        wait_bytes(rim_in.at[n, pl.ds(0, az - 1)], recv_e.at[n])
+        tiles = [rim_in[n, m] for m in range(az)] + [jnp.zeros((LANES - az, LANES), F32)]
+        return jnp.transpose(jnp.concatenate(tiles, axis=0))
 
     def speed_copy():
         return pltpu.make_async_remote_copy(
             speed_edge,
             speed_edge_in,
-            send_e.at[nf],
-            recv_e.at[nf],
+            send_e.at[nrims],
+            recv_e.at[nrims],
             device_id={"az": right, "rad": band},
             device_id_type=MESH,
         )
@@ -170,28 +191,42 @@
 
         lax.fori_loop(1, rad, to, 0)
 
-    def advect(i):
-        wait_bytes(edge_in.at[i], recv_e.at[i])
-        own_edge = edge[i]
-        from_left = pltpu.roll(edge_in[i, 0], 2, 1)
-        from_right = edge_in[i, 1]
-        speed_left = pltpu.roll(speed_edge_in[...], 2, 1)
-        first = pltpu.roll(own_edge, 1, 1)
-        entering = jnp.maximum(speed_left, 0.0) * from_left + jnp.minimum(speed_left, 0.0) * first
-        sides = jnp.where(jnp.bitwise_and(lane, 1) == 1, entering, from_right)
+    def advect(i, rims):
+        wait_bytes(arrived.at[i, pl.ds(0, rows - own)], recv_b.at[i])
+
+        def home(m, carry):
+            for j in range(own):
+                r = m * own + j
+                value = arrived[i, r]
+                rate, rate_back = speed[r], speed_back[r]
+                left, right = rims[2 * j], rims[2 * j + 1]
+                ahead = jnp.where(
+                    lane == LANES - 1, pltpu.roll(right, LANES - 1 - m, 1), pltpu.roll(value, LANES - 1, 1)
+                )
+                back = jnp.where(
+                    lane == 0, pltpu.roll(left, jnp.bitwise_and(LANES - m, LANES - 1), 1), pltpu.roll(value, 1, 1)
+                )
+                outflow = jnp.maximum(rate, 0.0) * value + jnp.minimum(rate, 0.0) * ahead
+                inflow = jnp.maximum(rate_back, 0.0) * back + jnp.minimum(rate_back, 0.0) * value
+                moved = value - (outflow - inflow)
+                if i == 0:
+                    energy[pl.ds(r, nth, stride=rows), :] = moved
+                else:
+                    out[order[i], pl.ds(r, nth, stride=rows), :] = moved
+            return carry
+
+        lax.fori_loop(0, az, home, 0, unroll=4)
+
+    def rims_of(table, place):
+        at = place * 2 * own * 8
+        return [table[at + 8 * c : at + 8 * (c + 1)] for c in range(2 * own)]
+
+    def back_speed():
+        wait_bytes(speed_edge_in, recv_e.at[nrims])
 
         def row(r, carry):
-            side = pltpu.roll(sides, LANES - 1 - 2 * r, 1)
-            value = arrived[i, r]
-            rate = speed[r]
-            ahead = jnp.where(lane == LANES - 1, side, pltpu.roll(value, LANES - 1, 1))
-            outflow = jnp.maximum(rate, 0.0) * value + jnp.minimum(rate, 0.0) * ahead
-            inflow = jnp.where(lane == 0, side, pltpu.roll(outflow, 1, 1))
-            moved = value - (outflow - inflow)
-            if i == 0:
-                energy[pl.ds(r, nth, stride=rows), :] = moved
-            else:
-                out[order[i], pl.ds(r, nth, stride=rows), :] = moved
+            entry = pltpu.roll(speed_edge_in[...], jnp.bitwise_and(LANES + 1 - 2 * r, LANES - 1), 1)
+            speed_back[r] = jnp.where(lane == 0, entry, pltpu.roll(speed[r], 1, 1))
             return carry
 
         lax.fori_loop(0, rows, row, 0, unroll=8)
@@ -276,35 +311,39 @@
     stage(0)
     pl.semaphore_wait(barrier, az - 1 + rad - 1)
     send_out(0)
-    stage(1)
-    send_out(1)
+    for i in range(1, nf - 1):
+        stage(i)
+        send_out(i)
     prepare()
-    for i in range(2, nf):
-        stage(i)
+    stage(nf - 1)
+    kept = []
     for i in range(nf):
-        rotate(i)
+        kept.append(rotate(i))
         send_home(i)
-        if i + 2 < nf:
-            send_out(i + 2)
+        if i == 0:
+            send_out(nf - 1)
+            send_rims(0, kept[0])
+        if i == nf - 2:
+            send_rims(1, sum(kept[1 : nf - 1], []))
+        if i == nf - 1:
+            send_rims(2, kept[nf - 1])
+        if i == 1:
+            back_speed()
         if i == 2:
-            wait_bytes(speed_edge_in, recv_e.at[nf])
-            advect(0)
+            advect(0, rims_of(take_rims(0), 0))
             solve_local()
-        if i == 4:
-            interface()
-        if i > 2:
-            advect(i - 2)
-        if i >= 1:
-            send_edges(i - 1)
-    send_edges(nf - 1)
-    advect(nf - 2)
-    advect(nf - 1)
+    table = take_rims(1)
+    for i in range(1, nf - 1):
+        advect(i, rims_of(table, i - 1))
+    interface()
+    advect(nf - 1, rims_of(take_rims(2), 0))
 
     for i in range(nf):
         wait_bytes(staged.at[i, pl.ds(0, rows - own)], send_a.at[i])
         wait_bytes(turned.at[i, pl.ds(0, az - 1)], send_b.at[i])
-        wait_bytes(edge_in.at[i], send_e.at[i])
-    wait_bytes(speed_edge, send_e.at[nf])
+    for n in range(nrims):
+        wait_bytes(rim.at[n, pl.ds(0, az - 1)], send_e.at[n])
+    wait_bytes(speed_edge, send_e.at[nrims])
     wait_bytes(corner_in.at[pl.ds(0, rad - 1)], send_r.at[0])
     wait_bytes(ends_in.at[pl.ds(0, rad - 1)], send_r.at[1])
 
@@ -331,10 +370,11 @@
             pltpu.VMEM((rows, nth, lanes), F32),
             pltpu.VMEM((whole, lanes), F32),
             pltpu.VMEM((nth, rows, lanes), F32),
-            pltpu.VMEM((nf, nth, lanes), F32),
-            pltpu.VMEM((nf, 2, nth, lanes), F32),
+            pltpu.VMEM((3, az, 1, lanes), F32),
+            pltpu.VMEM((3, az, 1, lanes), F32),
             pltpu.VMEM((nth, lanes), F32),
             pltpu.VMEM((nth, lanes), F32),
+            pltpu.VMEM((rows, nth, lanes), F32),
             pltpu.VMEM((nth, lanes), F32),
             pltpu.VMEM((rad, nth, lanes), F32),
             pltpu.VMEM((2, nth, lanes), F32),
@@ -348,14 +388,14 @@
             dma((nf,)),
             dma((nf,)),
             dma((nf,)),
-            dma((nf + 1,)),
-            dma((nf + 1,)),
+            dma((4,)),
+            dma((4,)),
             dma((2,)),
             dma((2,)),
         ]
         + [pltpu.VMEM((az, own, nth, lanes), F32)] * nf,
         compiler_params=pltpu.CompilerParams(
-            collective_id=0, has_side_effects=True, vmem_limit_bytes=40 << 20
+            collective_id=0, has_side_effects=True, vmem_limit_bytes=61 << 20
         ),
     )(
         fields.reshape(nf, whole, lanes),

time: 89.6 us -> 77.5 us (0.86)
  Pallas kernels: 83.8 us -> 74.8 us
  local copies, waits for them, and re-layouts: 5.58 us -> 2.52 us
    pallas_call x1, Pallas kernels: 83.8 us -> 74.8 us  [per_device(): pl.pallas_call(functools.partial(kernel, az, rad, nf, rows), out_shape=ja...]
    unnamed x11 -> x1, local copies, waits for them, and re-layouts: 5.58 us -> 2.52 us
where the time goes in v2:
time: 77.5 us; the launch traced here: 77.3 us
  Pallas kernels  74.8 us (97%)
  local copies, waits for them, and re-layouts  2.52 us (3%)
    pallas_call x1, Pallas kernels, per_device(): pl.pallas_call(functools.partial(kernel, az, rad, nf, rows), out_shape=ja...  74.8 us
    unnamed x1, local copies, waits for them, and re-layouts  2.52 us

profile of v2, /device:TPU:1, one launch (start us, length us, event | category | flops | bytes accessed | tf_op | source)
XLA Modules:
  0.0 77.3 jit_solution(12255670568601987180)
XLA Ops:
  0.0 74.8 %shard_map.55 = f32[5,512,128]{2,1,0:T(8,128)} custom-call(f32[5,512,128]{2,1,0:T(8,128)} %bitcast.5, f32[512,128]{1,0:T(8,128)} %bitcast.6, s32[64]{0:T(128)} %refs_2_.1, f32[8,64,64]{2,1,0:T(8,128)} %refs_3_.1, f32[8]{0:T(128)} %bitcast.7), custom_call_target="tpu_custom_call" | custom-call | tf_op jit(solution)/shard_map/pallas_call | solution.py:358
  74.8 2.5 %copy.7 = f32[5,8,64,128]{3,2,1,0:T(8,128)} copy(f32[5,8,64,128]{3,2,1,0:T(8,128)} %bitcast.4) | data formatting | bytes 2621440

commit v3 on v2

--- a/solution.py
+++ b/solution.py
@@ -215,7 +215,7 @@
                     out[order[i], pl.ds(r, nth, stride=rows), :] = moved
             return carry
 
-        lax.fori_loop(0, az, home, 0, unroll=4)
+        lax.fori_loop(0, az, home, 0, unroll=8)
 
     def rims_of(table, place):
         at = place * 2 * own * 8
@@ -319,14 +319,18 @@
     kept = []
     for i in range(nf):
         kept.append(rotate(i))
-        send_home(i)
         if i == 0:
+            send_rims(0, kept[0])
+            send_home(i)
             send_out(nf - 1)
-            send_rims(0, kept[0])
+        elif i < nf - 2:
+            send_home(i)
         if i == nf - 2:
             send_rims(1, sum(kept[1 : nf - 1], []))
+            send_home(i)
         if i == nf - 1:
             send_rims(2, kept[nf - 1])
+            send_home(i)
         if i == 1:
             back_speed()
         if i == 2:
@@ -395,14 +399,19 @@
         ]
         + [pltpu.VMEM((az, own, nth, lanes), F32)] * nf,
         compiler_params=pltpu.CompilerParams(
-            collective_id=0, has_side_effects=True, vmem_limit_bytes=61 << 20
+            collective_id=0, has_side_effects=True, vmem_limit_bytes=40 << 20
         ),
     )(
-        fields.reshape(nf, whole, lanes),
-        velocity.reshape(whole, lanes),
-        shifts,
-        block_inverse,
-        coupling.reshape(nth),
+        *(
+            pltpu.with_memory_space_constraint(x, pltpu.MemorySpace.HBM)
+            for x in (
+                fields.reshape(nf, whole, lanes),
+                velocity.reshape(whole, lanes),
+                shifts,
+                block_inverse,
+                coupling.reshape(nth),
+            )
+        )
     )
     return out.reshape(fields.shape)
 

time: 77.5 us -> 73.8 us (0.952)
  Pallas kernels: 74.8 us -> 72.7 us
  local copies, waits for them, and re-layouts: 2.52 us -> 1.06 us
    pallas_call x1, Pallas kernels: 74.8 us -> 72.7 us  [per_device(): pl.pallas_call(functools.partial(kernel, az, rad, nf, rows), out_shape=ja...]
    unnamed x1, local copies, waits for them, and re-layouts: 2.52 us -> 1.06 us
where the time goes in v3:
time: 73.8 us; the launch traced here: 73.7 us
  Pallas kernels  72.7 us (99%)
  local copies, waits for them, and re-layouts  1.06 us (1%)
    pallas_call x1, Pallas kernels, per_device(): pl.pallas_call(functools.partial(kernel, az, rad, nf, rows), out_shape=ja...  72.7 us

profile of v3, /device:TPU:1, one launch (start us, length us, event | category | flops | bytes accessed | tf_op | source)
XLA Modules:
  0.0 73.7 jit_solution(16179645455225304737)
XLA Ops:
  0.0 72.7 %shard_map.55 = f32[5,512,128]{2,1,0:T(8,128)S(1)} custom-call(f32[5,512,128]{2,1,0:T(8,128)} %bitcast.5, f32[512,128]{1,0:T(8,128)} %bitcast.6, s32[64]{0:T(128)} %refs_2_.1, f32[8,64,64]{2,1,0:T(8,128)} %refs_3_.1, f32[8]{0:T(128)} %bitcast.7), custom_call_target="tpu_custom_call" | custom-call | tf_op jit(solution)/shard_map/pallas_call | solution.py:362
  72.7 1.1 %copy.7 = f32[5,8,64,128]{3,2,1,0:T(8,128)} copy(f32[5,8,64,128]{3,2,1,0:T(8,128)S(1)} %bitcast.4) | data formatting | bytes 2621440

commit v4 on v3

--- a/solution.py
+++ b/solution.py
@@ -20,8 +20,7 @@
     nth = 8
     own = rows // az
     order = [nf - 1] + list(range(nf - 1))
-    groups = [[0], list(range(1, nf - 1)), [nf - 1]]
-    nrims = len(groups)
+    nrims = 2
     (f_hbm, v_hbm, shifts_hbm, g_hbm, link_hbm, out) = refs[:6]
     (raw, raw_v, g, staged, turned, arrived, speed, energy, local) = refs[6:15]
     (rim, rim_in, speed_edge, speed_edge_in, speed_back) = refs[15:20]
@@ -43,8 +42,7 @@
         pltpu.make_async_copy(shifts_hbm, shifts, par_sem.at[2]),
         pltpu.make_async_copy(link_hbm, link, par_sem.at[3]),
     ]
-    for copy in loads[:1] + params + loads[1:]:
-        copy.start()
+    loads[0].start()
 
     barrier = pltpu.get_barrier_semaphore()
 
@@ -58,6 +56,8 @@
 
     lax.fori_loop(1, az, greet_az, 0)
     lax.fori_loop(1, rad, greet_rad, 0)
+    for copy in loads[1:] + params:
+        copy.start()
 
     def stage(i):
         loads[i].wait()
@@ -320,27 +320,31 @@
     for i in range(nf):
         kept.append(rotate(i))
         if i == 0:
-            send_rims(0, kept[0])
             send_home(i)
             send_out(nf - 1)
+        elif i == 1:
+            send_rims(0, kept[0] + kept[1])
+            send_home(i)
         elif i < nf - 2:
             send_home(i)
         if i == nf - 2:
-            send_rims(1, sum(kept[1 : nf - 1], []))
             send_home(i)
         if i == nf - 1:
-            send_rims(2, kept[nf - 1])
+            send_rims(1, sum(kept[2:], []))
             send_home(i)
         if i == 1:
             back_speed()
-        if i == 2:
-            advect(0, rims_of(take_rims(0), 0))
+        if i == 3:
+            opened = take_rims(0)
+            advect(0, rims_of(opened, 0))
             solve_local()
+        if i == 3:
+            advect(1, rims_of(opened, 1))
     table = take_rims(1)
-    for i in range(1, nf - 1):
-        advect(i, rims_of(table, i - 1))
+    for i in range(2, nf - 1):
+        advect(i, rims_of(table, i - 2))
     interface()
-    advect(nf - 1, rims_of(take_rims(2), 0))
+    advect(nf - 1, rims_of(table, nf - 3))
 
     for i in range(nf):
         wait_bytes(staged.at[i, pl.ds(0, rows - own)], send_a.at[i])
@@ -374,8 +378,8 @@
             pltpu.VMEM((rows, nth, lanes), F32),
             pltpu.VMEM((whole, lanes), F32),
             pltpu.VMEM((nth, rows, lanes), F32),
-            pltpu.VMEM((3, az, 1, lanes), F32),
-            pltpu.VMEM((3, az, 1, lanes), F32),
+            pltpu.VMEM((2, az, 1, lanes), F32),
+            pltpu.VMEM((2, az, 1, lanes), F32),
             pltpu.VMEM((nth, lanes), F32),
             pltpu.VMEM((nth, lanes), F32),
             pltpu.VMEM((rows, nth, lanes), F32),
@@ -392,8 +396,8 @@
             dma((nf,)),
             dma((nf,)),
             dma((nf,)),
-            dma((4,)),
-            dma((4,)),
+            dma((3,)),
+            dma((3,)),
             dma((2,)),
             dma((2,)),
         ]

time: 73.8 us -> 73.3 us (level)
  no operation moved by 1% of the time
where the time goes in v4:
time: 73.3 us; the launch traced here: 73.2 us
  Pallas kernels  72.2 us (98%)
  local copies, waits for them, and re-layouts  1.06 us (1%)
    pallas_call x1, Pallas kernels, per_device(): pl.pallas_call(functools.partial(kernel, az, rad, nf, rows), out_shape=ja...  72.2 us

profile of v4, /device:TPU:1, one launch (start us, length us, event | category | flops | bytes accessed | tf_op | source)
XLA Modules:
  0.0 73.2 jit_solution(2862082490835234614)
XLA Ops:
  0.0 72.2 %shard_map.55 = f32[5,512,128]{2,1,0:T(8,128)S(1)} custom-call(f32[5,512,128]{2,1,0:T(8,128)} %bitcast.5, f32[512,128]{1,0:T(8,128)} %bitcast.6, s32[64]{0:T(128)} %refs_2_.1, f32[8,64,64]{2,1,0:T(8,128)} %refs_3_.1, f32[8]{0:T(128)} %bitcast.7), custom_call_target="tpu_custom_call" | custom-call | tf_op jit(solution)/shard_map/pallas_call | solution.py:366
  72.2 1.1 %copy.7 = f32[5,8,64,128]{3,2,1,0:T(8,128)} copy(f32[5,8,64,128]{3,2,1,0:T(8,128)S(1)} %bitcast.4) | data formatting | bytes 2621440

commit v5 on v4

--- a/solution.py
+++ b/solution.py
@@ -308,14 +308,12 @@
         corner_in[band] = table
         to_bands(corner, corner_in, 0, True)
 
-    stage(0)
+    for i in range(nf):
+        stage(i)
     pl.semaphore_wait(barrier, az - 1 + rad - 1)
-    send_out(0)
-    for i in range(1, nf - 1):
-        stage(i)
+    for i in range(nf - 1):
         send_out(i)
     prepare()
-    stage(nf - 1)
     kept = []
     for i in range(nf):
         kept.append(rotate(i))

time: 73.3 us -> 73.3 us (level)
  no operation moved by 1% of the time
where the time goes in v5:
time: 73.3 us; the launch traced here: 73.2 us
  Pallas kernels  72.2 us (98%)
  local copies, waits for them, and re-layouts  1.06 us (1%)
    pallas_call x1, Pallas kernels, per_device(): pl.pallas_call(functools.partial(kernel, az, rad, nf, rows), out_shape=ja...  72.2 us

profile of v5, /device:TPU:1, one launch (start us, length us, event | category | flops | bytes accessed | tf_op | source)
XLA Modules:
  0.0 73.2 jit_solution(4981808762706054287)
XLA Ops:
  0.0 72.2 %shard_map.55 = f32[5,512,128]{2,1,0:T(8,128)S(1)} custom-call(f32[5,512,128]{2,1,0:T(8,128)} %bitcast.5, f32[512,128]{1,0:T(8,128)} %bitcast.6, s32[64]{0:T(128)} %refs_2_.1, f32[8,64,64]{2,1,0:T(8,128)} %refs_3_.1, f32[8]{0:T(128)} %bitcast.7), custom_call_target="tpu_custom_call" | custom-call | tf_op jit(solution)/shard_map/pallas_call | solution.py:364
  72.2 1.1 %copy.7 = f32[5,8,64,128]{3,2,1,0:T(8,128)} copy(f32[5,8,64,128]{3,2,1,0:T(8,128)S(1)} %bitcast.4) | data formatting | bytes 2621440

commit v6 on v4

--- a/solution.py
+++ b/solution.py
@@ -21,6 +21,7 @@
     own = rows // az
     order = [nf - 1] + list(range(nf - 1))
     nrims = 2
+    half = az // 2
     (f_hbm, v_hbm, shifts_hbm, g_hbm, link_hbm, out) = refs[:6]
     (raw, raw_v, g, staged, turned, arrived, speed, energy, local) = refs[6:15]
     (rim, rim_in, speed_edge, speed_edge_in, speed_back) = refs[15:20]
@@ -117,19 +118,23 @@
         return [tile for j in range(own) for tile in done[j][1:]]
 
     def send_home(i):
-        def to(k, carry):
+        def to(k, carry, near=True):
             m = lax.rem(me + k, az)
             pltpu.make_async_remote_copy(
                 turned.at[i, m],
                 arrived.at[i, pl.ds(me * own, own)],
                 send_b.at[i],
-                recv_b.at[i],
+                recv_b.at[i if near else nf],
                 device_id={"az": m, "rad": band},
                 device_id_type=MESH,
             ).start()
             return carry
 
-        lax.fori_loop(1, az, to, 0)
+        if i == nf - 1:
+            lax.fori_loop(1, half, to, 0)
+            lax.fori_loop(half, az, functools.partial(to, near=False), 0)
+        else:
+            lax.fori_loop(1, az, to, 0)
         arrived[i, pl.ds(me * own, own)] = turned[i, me]
 
     key = jnp.bitwise_and(lax.shift_right_logical(lane + 1, 1), LANES // 2 - 1)
@@ -192,9 +197,8 @@
         lax.fori_loop(1, rad, to, 0)
 
     def advect(i, rims):
-        wait_bytes(arrived.at[i, pl.ds(0, rows - own)], recv_b.at[i])
-
-        def home(m, carry):
+        def home(k, carry):
+            m = lax.rem(me + az - k, az)
             for j in range(own):
                 r = m * own + j
                 value = arrived[i, r]
@@ -215,7 +219,14 @@
                     out[order[i], pl.ds(r, nth, stride=rows), :] = moved
             return carry
 
-        lax.fori_loop(0, az, home, 0, unroll=8)
+        if i == nf - 1:
+            wait_bytes(arrived.at[i, pl.ds(0, (half - 1) * own)], recv_b.at[i])
+            lax.fori_loop(0, half, home, 0, unroll=8)
+            wait_bytes(arrived.at[i, pl.ds(0, (az - half) * own)], recv_b.at[nf])
+            lax.fori_loop(half, az, home, 0, unroll=8)
+        else:
+            wait_bytes(arrived.at[i, pl.ds(0, rows - own)], recv_b.at[i])
+            lax.fori_loop(0, az, home, 0, unroll=8)
 
     def rims_of(table, place):
         at = place * 2 * own * 8
@@ -395,7 +406,7 @@
             dma((nf,)),
             dma((nf,)),
             dma((nf,)),
-            dma((nf,)),
+            dma((nf + 1,)),
             dma((3,)),
             dma((3,)),
             dma((2,)),

time: 73.3 us -> 73.3 us (level)
  no operation moved by 1% of the time
where the time goes in v6:
time: 73.3 us
  Pallas kernels  72.2 us (98%)
  local copies, waits for them, and re-layouts  1.06 us (1%)
    pallas_call x1, Pallas kernels, per_device(): pl.pallas_call(functools.partial(kernel, az, rad, nf, rows), out_shape=ja...  72.2 us

profile of v6, /device:TPU:1, one launch (start us, length us, event | category | flops | bytes accessed | tf_op | source)
XLA Modules:
  0.0 73.3 jit_solution(2541943576210772599)
XLA Ops:
  0.0 72.2 %shard_map.55 = f32[5,512,128]{2,1,0:T(8,128)S(1)} custom-call(f32[5,512,128]{2,1,0:T(8,128)} %bitcast.5, f32[512,128]{1,0:T(8,128)} %bitcast.6, s32[64]{0:T(128)} %refs_2_.1, f32[8,64,64]{2,1,0:T(8,128)} %refs_3_.1, f32[8]{0:T(128)} %bitcast.7), custom_call_target="tpu_custom_call" | custom-call | tf_op jit(solution)/shard_map/pallas_call | solution.py:377
  72.2 1.1 %copy.7 = f32[5,8,64,128]{3,2,1,0:T(8,128)} copy(f32[5,8,64,128]{3,2,1,0:T(8,128)S(1)} %bitcast.4) | data formatting | bytes 2621440
